TPU v7x, 256 devices: a whole 4x4x8 slice. The times are simulated.
256 devices in a mesh: ctx: 64 (over z, x, core), exp: 4 (over y).
Axes of the slice: x: 4, y: 4, z: 8, core: 2. Of those that a mesh axis runs over, the one named last changes fastest.
Arguments:
- tokens: bfloat16 [32768, 2048], P(('ctx', 'exp')), may hold values from -6 to 6
- norm_gain: float32 [2048], replicated, may hold values from 0.1 to 1.9
- w_query: bfloat16 [2048, 2048], P(None, 'exp'), may hold values from -0.125 to 0.125
- w_key: bfloat16 [2048, 2048], P(None, 'exp'), may hold values from -0.125 to 0.125
- w_value: bfloat16 [2048, 2048], P(None, 'exp'), may hold values from -0.125 to 0.125
- head_gain: float32 [2048], P('exp'), may hold values from 0.1 to 1.9
- w_out: bfloat16 [2048, 2048], P('exp'), may hold values from -0.125 to 0.125
- ffn_gain: float32 [2048], replicated, may hold values from 0.1 to 1.9
- indices: int32 [32768, 2], P(('ctx', 'exp')), may hold values from 0 to 63, all different within a row; in each aligned block of 128 rows (0 to 127, 128 to 255, ...) at most 5 rows name the same one
- gates: bfloat16 [32768, 2], P(('ctx', 'exp')), may hold values from 0.049804688 to 1
- w_gate: bfloat16 [64, 2048, 1024], P('ctx', None, 'exp'), may hold values from -0.125 to 0.125
- w_up: bfloat16 [64, 2048, 1024], P('ctx', None, 'exp'), may hold values from -0.125 to 0.125
- w_down: bfloat16 [64, 2048, 1024], P('ctx', None, 'exp'), may hold values from -0.1875 to 0.1875
Outputs:
- mixed: bfloat16 [32768, 2048], P(('ctx', 'exp'))
Inputs may be any that keep to these rules, and one draw needn't show every extreme that they name: `indices`: the two entries of a row differ. In the rows of one device no expert is named more than 5 times, and in some device's rows some expert is named exactly 5 times.
All inputs are finite; a program needn't handle non-finite values.
Results may differ from a plain program's by a relative error of at most 0.015.
Values may be sent and summed in bfloat16 or wider, within the bound.
A program may use at most 128 MiB of HBM per device.

v0:
```python
import jax
import jax.numpy as jnp
from jax import lax
from jax.sharding import PartitionSpec as P

HD = 128
BLK = 512


epsilon = 1e-06


def carried_in(array, axis, join, neutral):
    place = lax.axis_index(axis)
    gathered = lax.all_gather(array.astype(jnp.bfloat16), axis)
    state = jnp.zeros_like(array) + jnp.asarray(neutral, array.dtype)

    def one(turn, state):
        return join(state, lax.dynamic_index_in_dim(gathered, turn, 0, False).astype(array.dtype))

    return lax.fori_loop(0, place, one, state)


def rms_rows(values, gain):
    widened = values.astype(jnp.float32)
    mean_square = jnp.mean(widened * widened, axis=-1, keepdims=True)
    return widened * lax.rsqrt(mean_square + epsilon) * gain


def rounded(values):
    return lax.optimization_barrier(values.astype(jnp.bfloat16)).astype(jnp.float32)


def block_slots(picked, expert_count, capacity):
    flat_ids = picked.reshape(-1)
    chosen = (flat_ids[:, None] == jnp.arange(expert_count, dtype=jnp.int32)[None, :]).astype(
        jnp.int32
    )
    earlier = jnp.cumsum(chosen, axis=0) - chosen
    position = jnp.sum(earlier * chosen, axis=1)
    return (flat_ids * capacity + position).reshape(picked.shape)


def add_states(earlier, later):
    return earlier + later


def on_device(
    tokens,
    norm_gain,
    w_query,
    w_key,
    w_value,
    head_gain,
    w_out,
    ffn_gain,
    indices,
    gates,
    w_gate,
    w_up,
    w_down,
):
    tok_rows, model_width = tokens.shape
    ctx_count = lax.axis_size("ctx")
    local_experts = w_gate.shape[0]
    expert_count = local_experts * ctx_count
    capacity = max(2, (5 * tok_rows + 2 * expert_count - 1) // (2 * expert_count))
    normed = rms_rows(tokens, norm_gain).astype(jnp.bfloat16)
    joined_weights = jnp.concatenate([w_query, w_key, w_value], axis=1)
    projected = jnp.dot(
        lax.all_gather(normed, "exp", axis=0, tiled=True),
        joined_weights,
        preferred_element_type=jnp.float32,
    ).astype(jnp.bfloat16)
    shard_rows = projected.shape[0]
    local_width = w_query.shape[1]
    local_heads = local_width // HD
    block_count = shard_rows // BLK

    def split_heads(columns):
        return columns.reshape(block_count, BLK, local_heads, HD).transpose(0, 2, 1, 3)

    query_blocks = split_heads(projected[:, :local_width])
    key_blocks = split_heads(projected[:, local_width : 2 * local_width])
    value_blocks = split_heads(projected[:, 2 * local_width :])
    causal = jnp.tril(jnp.ones((BLK, BLK), dtype=bool))

    def block_step(kv_state, block):
        query_block, key_block, value_block = block
        score_block = jnp.einsum(
            "hqd,hkd->hqk", query_block, key_block, preferred_element_type=jnp.float32
        )
        masked = jnp.where(causal[None], score_block, 0.0).astype(jnp.bfloat16)
        inside = jnp.einsum("hqk,hkd->hqd", masked, value_block, preferred_element_type=jnp.float32)
        carried = jnp.einsum(
            "hqd,hde->hqe",
            query_block.astype(jnp.float32),
            kv_state,
            precision=lax.Precision.HIGHEST,
        )
        kv_state = kv_state + jnp.einsum(
            "hkd,hke->hde", key_block, value_block, preferred_element_type=jnp.float32
        )
        return (kv_state, inside + carried)

    local_state, inside_rows = lax.scan(
        block_step,
        jnp.zeros((local_heads, HD, HD), jnp.float32),
        (query_blocks, key_blocks, value_blocks),
    )
    before = carried_in(local_state, "ctx", add_states, jnp.zeros_like(local_state))
    carried_rows = jnp.einsum(
        "bhqd,hde->bhqe", query_blocks.astype(jnp.float32), before, precision=lax.Precision.HIGHEST
    )
    attended = inside_rows + carried_rows
    mean_square = jnp.mean(attended * attended, axis=-1, keepdims=True)
    head_out = (
        attended * lax.rsqrt(mean_square + epsilon) * head_gain.reshape(1, local_heads, 1, HD)
    ).astype(jnp.bfloat16)
    head_rows = head_out.transpose(0, 2, 1, 3).reshape(shard_rows, local_width)
    part = head_rows
    head_total = lax.psum_scatter(
        rounded(jnp.dot(part, w_out, preferred_element_type=jnp.float32)).astype(jnp.bfloat16),
        "exp",
        scatter_dimension=0,
        tiled=True,
    ).astype(jnp.float32)
    residual_rows = (tokens.astype(jnp.float32) + head_total).astype(jnp.bfloat16)
    moe_in = rms_rows(residual_rows, ffn_gain).astype(jnp.bfloat16)
    slots = block_slots(indices, expert_count, capacity)
    slot_ids = jnp.arange(expert_count * capacity, dtype=jnp.int32)
    matched = slot_ids[:, None, None] == slots[None]
    dispatch_table = jnp.any(matched, axis=2).astype(jnp.bfloat16)
    combine_table = jnp.sum(
        jnp.where(matched, gates[None].astype(jnp.float32), 0.0), axis=2
    ).T.astype(jnp.bfloat16)
    outgoing = jnp.dot(dispatch_table, moe_in, preferred_element_type=jnp.float32).astype(
        jnp.bfloat16
    )
    outgoing = outgoing.reshape(ctx_count, local_experts, capacity, model_width)
    piece = lax.all_gather(
        lax.all_to_all(outgoing, "ctx", split_axis=0, concat_axis=0, tiled=True)[None],
        "exp",
        axis=0,
        tiled=True,
    )
    gate_rows = jnp.einsum("xsepd,edf->xsepf", piece, w_gate, preferred_element_type=jnp.float32)
    up_rows = jnp.einsum("xsepd,edf->xsepf", piece, w_up, preferred_element_type=jnp.float32)
    hidden_rows = (jax.nn.silu(gate_rows) * up_rows).astype(jnp.bfloat16)
    part = hidden_rows
    summed = lax.psum_scatter(
        rounded(
            jnp.einsum("xsepf,edf->xsepd", part, w_down, preferred_element_type=jnp.float32)
        ).astype(jnp.bfloat16),
        "exp",
        scatter_dimension=0,
        tiled=True,
    ).astype(jnp.float32)
    expert_rows_out = summed[0].astype(jnp.bfloat16)
    returned = lax.all_to_all(expert_rows_out, "ctx", split_axis=0, concat_axis=0, tiled=True)
    returned = returned.reshape(expert_count * capacity, model_width)
    moe_total = jnp.dot(combine_table, returned, preferred_element_type=jnp.float32)
    return (residual_rows.astype(jnp.float32) + moe_total).astype(jnp.bfloat16)


def solution(mesh):
    placed = (
        P(("ctx", "exp"), None),
        P(),
        P(None, "exp"),
        P(None, "exp"),
        P(None, "exp"),
        P("exp"),
        P("exp", None),
        P(),
        P(("ctx", "exp"), None),
        P(("ctx", "exp"), None),
        P("ctx", None, "exp"),
        P("ctx", None, "exp"),
        P("ctx", None, "exp"),
    )
    return jax.shard_map(
        on_device, mesh=mesh, in_specs=placed, out_specs=P(("ctx", "exp"), None), check_vma=False
    )
```

profile of v0, /device:TPU:39, one launch (start us, length us, event | category | flops | bytes accessed | tf_op | source)
XLA Modules:
  0.0 511.9 jit_solution(7972014715759821155)
XLA Ops:
  6.5 1.4 fusion.33
  7.9 2.0 fusion.35
  10.0 35.8 %all-gather.6.cloned.1.call-done = bf16[512,2048]{1,0:T(8,128)(2,1)} async-done(((bf16[128,2048]{1,0:T(8,128)(2,1)}), bf16[512,2048]{1,0:T(8,128)(2,1)}) %all-gather.6.cloned.1.call-update) | async-done | bytes 2097168 | tf_op jit(solution)/shard_map/all_gather | solution.py:71
  45.9 6.9 %fusion.10 = bf16[512,1536]{1,0:T(8,128)(2,1)S(1)} fusion(bf16[512,2048]{1,0:T(8,128)(2,1)} %all-gather.6.cloned.1.call-done, bf16[2048,512]{1,0:T(8,128)(2,1)} %param.19, bf16[2048,512]{1,0:T(8,128)(2,1)} %param.18, bf16[2048,512]{1,0:T(8,128)(2,1)} %param.17), kind=kOutput, calls=%fused_computation.13 | convolution fusion | flops 3240886272 | bytes 9961472 | tf_op jit(solution)/shard_map/dot_general | solution.py:70
  52.7 1.1 fusion.78
  54.1 1.2 reshape.124
  55.3 1.0 convolution_convert_fusion.2
  56.4 0.8 iota_compare_fusion
  57.1 1.2 reshape.123
  58.4 1.6 fusion.53
  60.0 3.8 fusion.25
  63.8 74.0 %all-gather.8.cloned.1.call-done = bf16[256,128,128]{2,1,0:T(8,128)(2,1)} async-done(((bf16[4,128,128]{2,1,0:T(8,128)(2,1)}), bf16[256,128,128]{2,1,0:T(8,128)(2,1)}) %all-gather.8.cloned.1.call-update) | async-done | bytes 8388624 | tf_op jit(solution)/shard_map/all_gather | solution.py:15
  137.8 14.9 %while.2 = (s32[]{:T(128)}, f32[4,128,128]{2,1,0:T(8,128)S(1)}, s32[]{:T(128)}, bf16[64,4,128,128]{3,2,1,0:T(8,128)(2,1)}, s32[]{:T(128)}, /*index=5*/s32[]{:T(128)}, s32[]{:T(128)}) while((s32[]{:T(128)}, f32[4,128,128]{2,1,0:T(8,128)S(1)}, s32[]{:T(128)}, bf16[64,4,128,128]{3,2,1,0:T(8,128)(2,1)}, s32[]{:T(128)}, /*index=5*/s32[]{:T(128)}, ...), condition=%wide.region_2.3_spmd, body=%wide.region_1.2_spmd.sunk | while | flops 131077 | bytes 655475 | solution.py:21
  137.9 1.0 convert_add_fusion.3
  138.9 1.0 convert_add_fusion.3
  139.8 1.0 convert_add_fusion.3
  140.8 1.0 convert_add_fusion.3
  141.8 1.0 convert_add_fusion.3
  142.8 1.0 convert_add_fusion.3
  143.8 1.0 convert_add_fusion.3
  144.8 1.0 convert_add_fusion.3
  145.8 1.0 convert_add_fusion.3
  146.8 1.0 convert_add_fusion.3
  147.8 1.0 convert_add_fusion.3
  148.8 1.0 convert_add_fusion.3
  149.8 1.0 convert_add_fusion.3
  150.7 1.0 convert_add_fusion.3
  151.7 1.0 convert_add_fusion.3
  152.7 1.9 multiply_reduce_fusion
  154.8 2.6 convolution_convert_fusion
  157.5 0.6 copy-done.6
  158.6 0.6 reduce-window.6
  159.8 74.6 %reduce-scatter.3.cloned.1.call-done = bf16[128,2048]{1,0:T(8,128)(2,1)} async-done(((bf16[512,2048]{1,0:T(8,128)(2,1)}), bf16[128,2048]{1,0:T(8,128)(2,1)}) %reduce-scatter.3.cloned.1.call-update) | async-done | bytes 524304 | tf_op jit(solution)/shard_map/reduce_scatter | solution.py:122
  234.4 1.3 fusion.37
  235.7 2.7 convolution_convert_fusion.1
  238.4 3.4 reshape.128
  241.8 60.5 %all_to_all.10 = bf16[64,1,5,2048]{3,2,1,0:T(8,128)(2,1)S(1)} all-to-all(bf16[64,1,5,2048]{3,2,1,0:T(8,128)(2,1)} %bitcast.129), channel_id=1, replica_groups=mesh['ctx'=64,'exp'=4] {'ctx'}, dimensions={0} | all-to-all | bytes 2621440 | tf_op jit(solution)/shard_map/all_to_all | solution.py:142
  302.3 2.0 copy.86
  304.3 0.2 reduce-scatter.5.cloned.1.call-start
  304.5 55.2 %all-gather.10.cloned.1.call-done = bf16[256,1,5,2048]{3,0,2,1:T(8,128)(2,1)} async-done(((bf16[64,1,5,2048]{3,0,2,1:T(8,128)(2,1)}), bf16[256,1,5,2048]{3,0,2,1:T(8,128)(2,1)}) %all-gather.10.cloned.1.call-update) | async-done | bytes 5242896 | tf_op jit(solution)/shard_map/all_gather | solution.py:141
  359.7 5.4 %fusion.15 = f32[4,64,1,5,256]{4,1,3,0,2:T(8,128)} fusion(bf16[4,64,5,2048]{3,1,0,2:T(8,128)(2,1)} %bitcast.136, bf16[1,2048,256]{2,1,0:T(8,128)(2,1)} %param.25), kind=kOutput, calls=%fused_computation.24 | convolution fusion | flops 1342177280 | bytes 7602176 | tf_op jit(solution)/shard_map/xsepd,edf->xsepf/dot_general | solution.py:147
  365.1 11.2 %convert_bitcast_fusion = bf16[4,64,1,5,2048]{4,1,3,0,2:T(8,128)(2,1)} fusion(bf16[1,2048,256]{2,1,0:T(8,128)(2,1)} %param.27, bf16[4,64,5,2048]{3,1,0,2:T(8,128)(2,1)} %bitcast.137, f32[4,64,1,5,256]{4,1,3,0,2:T(8,128)} %fusion.15, bf16[1,2048,256]{2,1,0:T(8,128)(2,1)} %param.26), kind=kOutput, calls=%fused_computation.7 | convolution fusion | flops 2688942080 | bytes 13893632 | tf_op jit(solution)/shard_map/xsepf,edf->xsepd/dot_general | solution.py:153
  376.3 58.7 %reduce-scatter.5.cloned.1.call-done = bf16[1,64,1,5,2048]{4,1,3,0,2:T(8,128)(2,1)} async-done(((bf16[4,64,1,5,2048]{4,1,3,0,2:T(8,128)(2,1)}), bf16[1,64,1,5,2048]{4,1,3,0,2:T(8,128)(2,1)}) %reduce-scatter.5.cloned.1.call-update) | async-done | bytes 1310736 | tf_op jit(solution)/shard_map/reduce_scatter | solution.py:151
  435.0 3.4 copy.89
  438.4 11.1 %all-to-all-start.1 = ((bf16[64,1,5,2048]{3,2,1,0:T(8,128)(2,1)}), bf16[64,1,5,2048]{3,2,1,0:T(8,128)(2,1)}, u32[]{:S(2)}, u32[]{:S(2)}) async-start(bf16[64,1,5,2048]{3,2,1,0:T(8,128)(2,1)} %copy.89), calls=%async_computation.3 | async-start | bytes 4194304 | tf_op jit(solution)/shard_map/all_to_all | solution.py:160
  449.6 49.6 %all-to-all-done.1 = bf16[64,1,5,2048]{3,2,1,0:T(8,128)(2,1)} async-done(((bf16[64,1,5,2048]{3,2,1,0:T(8,128)(2,1)}), bf16[64,1,5,2048]{3,2,1,0:T(8,128)(2,1)}, u32[]{:S(2)}, u32[]{:S(2)}) %all-to-all-start.1) | async-done | bytes 1310752 | tf_op jit(solution)/shard_map/all_to_all | solution.py:160
  499.2 3.7 reshape.134
  502.8 2.6 fusion.13
  (46 shorter events, 1.7 us)
Async XLA Ops:
  6.5 148.3 %copy-start = (bf16[512,2048]{1,0:T(8,128)(2,1)S(1)}, bf16[512,2048]{1,0:T(8,128)(2,1)}, u32[]{:S(2)}) copy-start(bf16[512,2048]{1,0:T(8,128)(2,1)} %param.21) | copy-start | bytes 6291460
  6.5 39.3 %all-gather.6.cloned.1.call-start = ((), (), s32[]{:S(2)}) async-start(), calls=%async_computation.4 | async-start | bytes 2621440 | tf_op jit(solution)/shard_map/all_gather | solution.py:71
  10.0 127.8 %all-gather.8.cloned.1.call-start = ((), (), s32[]{:S(2)}) async-start(), calls=%async_computation.7 | async-start | bytes 8519680 | tf_op jit(solution)/shard_map/all_gather | solution.py:15
  55.3 1.9 copy-start.3
  56.3 178.1 %reduce-scatter.3.cloned.1.call-start = ((), (), s32[]{:S(2)}) async-start(), calls=%async_computation.5 | async-start | bytes 2621440 | tf_op jit(solution)/shard_map/reduce_scatter | solution.py:122
  57.1 2.9 copy-start.4
  152.7 1.9 copy-start.7
  157.5 0.7 copy-start.6
  157.5 76.9 %copy-start.1 = (bf16[128,2048]{1,0:T(8,128)(2,1)S(1)}, bf16[128,2048]{1,0:T(8,128)(2,1)}, u32[]{:S(2)}) copy-start(bf16[128,2048]{1,0:T(8,128)(2,1)} %param.15) | copy-start | bytes 1572868
  157.5 78.2 %copy-start.5 = (f32[2048]{0:T(1024)S(1)}, f32[2048]{0:T(1024)}, u32[]{:S(2)}) copy-start(f32[2048]{0:T(1024)} %param.22) | copy-start | bytes 24580
  157.5 202.2 %all-gather.10.cloned.1.call-start = ((), (), s32[]{:S(2)}) async-start(), calls=%async_computation.8 | async-start | bytes 6553600 | tf_op jit(solution)/shard_map/all_gather | solution.py:141
  304.3 130.7 %reduce-scatter.5.cloned.1.call-start = ((), (), s32[]{:S(2)}) async-start(), calls=%async_computation.6 | async-start | bytes 6553600 | tf_op jit(solution)/shard_map/reduce_scatter | solution.py:151
  438.4 11.1 %copy-start.8 = (bf16[128,2]{0,1:T(2,128)(2,1)S(1)}, bf16[128,2]{0,1:T(2,128)(2,1)}, u32[]{:S(2)}) copy-start(bf16[128,2]{0,1:T(2,128)(2,1)} %param.24) | copy-start | bytes 1540
  438.4 60.8 %all-to-all-start.1 = ((bf16[64,1,5,2048]{3,2,1,0:T(8,128)(2,1)}), bf16[64,1,5,2048]{3,2,1,0:T(8,128)(2,1)}, u32[]{:S(2)}, u32[]{:S(2)}) async-start(bf16[64,1,5,2048]{3,2,1,0:T(8,128)(2,1)} %copy.89), calls=%async_computation.3 | async-start | bytes 4194304 | tf_op jit(solution)/shard_map/all_to_all | solution.py:160
  449.5 53.3 %copy-start.2 = (bf16[128,2048]{1,0:T(8,128)(2,1)S(1)}, bf16[128,2048]{1,0:T(8,128)(2,1)}, u32[]{:S(2)}) copy-start(bf16[128,2048]{1,0:T(8,128)(2,1)} %reduce-scatter.3.cloned.1.call-done) | copy-start | bytes 1572868
Sparse Core Ops, SparseCore 0:
  10.1 35.7 all-gather.5
  56.4 81.3 all-gather.7
  157.6 76.7 reduce-scatter.2
  304.4 55.2 all-gather.9
  376.4 58.5 reduce-scatter.4
where the time goes:
time: 516 us; the launch traced here: 512 us
  waiting for transfers between devices  348 us (67%)
  blocking collectives  60.5 us (12%)
  matrix products  39.7 us (8%)
  other arithmetic  21 us (4%)
  local copies, waits for them, and re-layouts  17.5 us (3%)
  between operations  13.3 us (3%)
  starting transfers between devices  11.4 us (2%)
    reduce_scatter x1, waiting for transfers between devices, on_device(): lax.psum_scatter(rounded(jnp.dot(part, w_out, preferred_element_type=jnp....  74.6 us
    all_gather x1, waiting for transfers between devices, carried_in(): gathered = lax.all_gather(array.astype(jnp.bfloat16), axis)  74 us
    all_to_all x1, blocking collectives, on_device(): lax.all_to_all(outgoing, 'ctx', split_axis=0, concat_axis=0, tiled=True)  60.5 us
    reduce_scatter x1, waiting for transfers between devices, on_device(): lax.psum_scatter(rounded(jnp.einsum('xsepf,edf->xsepd', part, w_down, pre...  58.7 us
    all_gather x1, waiting for transfers between devices, on_device(): lax.all_gather(lax.all_to_all(outgoing, 'ctx', split_axis=0, concat_axis=...  55.2 us
    all_to_all x1, waiting for transfers between devices, on_device(): lax.all_to_all(expert_rows_out, 'ctx', split_axis=0, concat_axis=0, tiled...  49.6 us
    all_gather x1, waiting for transfers between devices, on_device(): lax.all_gather(normed, 'exp', axis=0, tiled=True)  35.8 us
    add x15, other arithmetic, add_states(): return earlier + later  14.5 us
  transfers between devices with their start and end apart: 6, of which 6 were waited for; matrix products, arithmetic and copies ran while one was open for 2% of the time, Pallas kernels for 0%

commit v1 on v0

--- a/solution.py
+++ b/solution.py
@@ -1,10 +1,16 @@
+import functools
+
 import jax
 import jax.numpy as jnp
 from jax import lax
+from jax.experimental import pallas as pl
+from jax.experimental.pallas import tpu as pltpu
 from jax.sharding import PartitionSpec as P
 
 HD = 128
 BLK = 512
+LANES = 128
+MESH = pl.DeviceIdType.MESH
 
 
 epsilon = 1e-06
@@ -43,6 +49,330 @@
 
 def add_states(earlier, later):
     return earlier + later
+
+
+def ctx_grid(count):
+    members = 8 if count % 8 == 0 and count > 8 else count // 2
+    return count // members, members
+
+
+def routing(indices, expert_count, capacity, planes, members):
+    rows, picks = indices.shape
+    flat = indices.reshape(-1)
+    count = flat.shape[0]
+    number = jnp.arange(count, dtype=jnp.int32)
+    same = (flat[:, None] == flat[None, :]) & (number[None, :] < number[:, None])
+    position = jnp.sum(same.astype(jnp.int32), axis=1)
+    away = jnp.mod(lax.axis_index("ctx") // members - flat // members + planes, planes)
+    turn = jnp.where(
+        away == 0, 0, jnp.where(away <= planes // 2, 2 * away - 1, 2 * (planes - away))
+    )
+    slot_of = (turn * members + flat % members) * capacity + position
+    slot_ids = jnp.arange(expert_count * capacity, dtype=jnp.int32)
+    token_of = jnp.sum(
+        jnp.where(slot_ids[:, None] == slot_of[None, :], (number // picks)[None, :], 0), axis=1
+    )
+    return slot_of.astype(jnp.int32), token_of.astype(jnp.int32)
+
+
+def relative_order(planes):
+    order = [0]
+    for far in range(1, planes // 2 + 1):
+        order.append(far)
+        if len(order) < planes:
+            order.append(planes - far)
+    return order
+
+
+def expert_kernel(
+    planes,
+    members,
+    ring,
+    capacity,
+    moe_ref,
+    resid_ref,
+    token_ref,
+    slot_ref,
+    gate_ref,
+    wg_hbm,
+    wu_hbm,
+    wd_hbm,
+    wdall_hbm,
+    out_ref,
+    sent,
+    got,
+    rows,
+    hidden_out,
+    hidden_in,
+    answer,
+    back,
+    wgu,
+    wd,
+    local_sem,
+    weight_sem,
+    out_sem,
+    in_sem,
+    ring_send,
+    ring_recv,
+    hid_send,
+    hid_recv,
+    ret_send,
+    ret_recv,
+):
+    here = lax.axis_index("ctx")
+    y = lax.axis_index("exp")
+    z, m = here // members, here % members
+    right, left, across = (y + 1) % ring, (y + ring - 1) % ring, (y + 2) % ring
+    cell = capacity
+    plane_rows = members * cell
+    chunk_rows = 2 * plane_rows
+    chunks = planes // 2
+    order = relative_order(planes)
+    half = wgu.shape[0] // 2
+    width = wg_hbm.shape[1]
+
+    loads = [
+        pltpu.make_async_copy(wg_hbm, wgu.at[:, pl.ds(0, width)], weight_sem.at[0]),
+        pltpu.make_async_copy(wu_hbm, wgu.at[:, pl.ds(width, width)], weight_sem.at[1]),
+        pltpu.make_async_copy(wd_hbm, wd.at[y], weight_sem.at[2]),
+    ]
+    for step in range(1, ring):
+        other = (y + step) % ring
+        loads.append(
+            pltpu.make_async_copy(wdall_hbm.at[other], wd.at[other], weight_sem.at[2 + step])
+        )
+    for load in loads:
+        load.start()
+
+    barrier = pltpu.get_barrier_semaphore()
+    everyone = planes * members
+
+    def greet(step, carry):
+        pl.semaphore_signal(
+            barrier, inc=1, device_id=((here + step) % everyone, y), device_id_type=MESH
+        )
+        return carry
+
+    lax.fori_loop(1, everyone, greet, 0)
+    for step in range(1, ring):
+        pl.semaphore_signal(
+            barrier, inc=1, device_id=(here, (y + step) % ring), device_id_type=MESH
+        )
+
+    def pick(slot, carry):
+        sent[slot] = moe_ref[token_ref[slot]]
+        return carry
+
+    def to_plane(k):
+        def one(step, carry):
+            t = (m + step) % members
+            pltpu.make_async_remote_copy(
+                src_ref=sent.at[pl.ds(k * plane_rows + t * cell, cell)],
+                dst_ref=got.at[pl.ds(k * plane_rows + m * cell, cell)],
+                send_sem=out_sem,
+                recv_sem=in_sem.at[k // 2],
+                device_id=(((z + planes - order[k]) % planes) * members + t, y),
+                device_id_type=MESH,
+            ).start()
+            return carry
+
+        return one
+
+    for k in range(planes):
+        lax.fori_loop(k * plane_rows, (k + 1) * plane_rows, pick, 0, unroll=8)
+        if k == 0:
+            pl.semaphore_wait(barrier, everyone - 1 + ring - 1)
+            own = pl.ds(m * cell, cell)
+            pltpu.make_async_copy(sent.at[own], got.at[own], in_sem.at[0]).start()
+            lax.fori_loop(1, members, to_plane(k), 0)
+        else:
+            lax.fori_loop(0, members, to_plane(k), 0)
+
+    def ring_copy(owner, c, columns, target, kind):
+        piece = rows.at[owner, pl.ds(c * chunk_rows, chunk_rows), columns]
+        return pltpu.make_async_remote_copy(
+            src_ref=piece,
+            dst_ref=piece,
+            send_sem=ring_send.at[kind, c],
+            recv_sem=ring_recv.at[kind, c],
+            device_id=(here, target),
+            device_id_type=MESH,
+        )
+
+    everything, low, high = pl.ds(0, 2 * half), pl.ds(0, half), pl.ds(half, half)
+
+    def own_chunk(c):
+        part = pl.ds(c * chunk_rows, chunk_rows)
+        pltpu.make_async_copy(got.at[part], got.at[part], in_sem.at[c]).wait()
+        rows[y, part, :] = got[part].reshape(chunk_rows, 2 * half)
+        ring_copy(y, c, everything, right, 0).start()
+        ring_copy(y, c, everything, left, 1).start()
+
+    def pass_on(c):
+        ring_copy(left, c, everything, right, 0).wait_recv()
+        ring_copy(left, c, low, right, 2).start()
+        ring_copy(right, c, everything, left, 1).wait_recv()
+        ring_copy(right, c, high, left, 3).start()
+
+    def hidden_copy(c, target):
+        step = lax.rem(target - y + ring, ring)
+        return pltpu.make_async_remote_copy(
+            src_ref=hidden_out.at[c, target],
+            dst_ref=hidden_in.at[c, y],
+            send_sem=hid_send.at[c, step],
+            recv_sem=hid_recv.at[c, step],
+            device_id=(here, target),
+            device_id_type=MESH,
+        )
+
+    def hidden_arrival(c, source):
+        step = lax.rem(y - source + ring, ring)
+        return pltpu.make_async_remote_copy(
+            src_ref=hidden_out.at[c, source],
+            dst_ref=hidden_in.at[c, source],
+            send_sem=hid_send.at[c, step],
+            recv_sem=hid_recv.at[c, step],
+            device_id=(here, source),
+            device_id_type=MESH,
+        )
+
+    def expand(c):
+        ring_copy(across, c, low, right, 2).wait_recv()
+        ring_copy(across, c, high, left, 3).wait_recv()
+        part = pl.ds(c * chunk_rows, chunk_rows)
+        block = rows[:, part, :].reshape(ring * chunk_rows, 2 * half)
+        both = jnp.dot(block, wgu[...], preferred_element_type=jnp.float32)
+        gate_rows, up_rows = both[:, :width], both[:, width:]
+        hidden = (gate_rows / (1.0 + jnp.exp(-gate_rows)) * up_rows).astype(jnp.bfloat16)
+        hidden_out[c] = hidden.reshape(ring, chunk_rows, width)
+        for step in range(1, ring):
+            hidden_copy(c, (y + step) % ring).start()
+        hidden_in[c, y] = hidden_out[c, y]
+
+    def contract(c):
+        for step in range(1, ring):
+            hidden_arrival(c, (y + step) % ring).wait_recv()
+        total = None
+        for g in range(ring):
+            term = lax.dot_general(
+                hidden_in[c, g],
+                wd[g],
+                (((1,), (1,)), ((), ())),
+                preferred_element_type=jnp.float32,
+            )
+            total = term if total is None else total + term
+        part = pl.ds(c * chunk_rows, chunk_rows)
+        answer[part] = total.astype(jnp.bfloat16).reshape(chunk_rows, *answer.shape[1:])
+        for k in (2 * c, 2 * c + 1):
+
+            def one(step, carry):
+                t = (m + step) % members
+                pltpu.make_async_remote_copy(
+                    src_ref=answer.at[pl.ds(k * plane_rows + t * cell, cell)],
+                    dst_ref=back.at[pl.ds(k * plane_rows + m * cell, cell)],
+                    send_sem=ret_send,
+                    recv_sem=ret_recv,
+                    device_id=(((z + order[k]) % planes) * members + t, y),
+                    device_id_type=MESH,
+                ).start()
+                return carry
+
+            if k == 0:
+                own = pl.ds(m * cell, cell)
+                pltpu.make_async_copy(answer.at[own], back.at[own], ret_recv).start()
+                lax.fori_loop(1, members, one, 0)
+            else:
+                lax.fori_loop(0, members, one, 0)
+
+    for c in range(chunks + 3):
+        if c < chunks:
+            own_chunk(c)
+        if 0 <= c - 1 < chunks:
+            pass_on(c - 1)
+        if c - 2 == 0:
+            loads[0].wait()
+            loads[1].wait()
+        if 0 <= c - 2 < chunks:
+            expand(c - 2)
+        if c - 3 == 0:
+            for load in loads[2:]:
+                load.wait()
+        if 0 <= c - 3 < chunks:
+            contract(c - 3)
+
+    total_rows = planes * plane_rows
+    pltpu.make_async_copy(back, back, ret_recv).wait()
+
+    def blend(t, carry):
+        mixed = (
+            resid_ref[t].astype(jnp.float32)
+            + gate_ref[2 * t] * back[slot_ref[2 * t]].astype(jnp.float32)
+            + gate_ref[2 * t + 1] * back[slot_ref[2 * t + 1]].astype(jnp.float32)
+        )
+        out_ref[t] = mixed.astype(jnp.bfloat16)
+        return carry
+
+    lax.fori_loop(0, out_ref.shape[0], blend, 0, unroll=4)
+
+    sent_away = pl.ds(0, total_rows - cell)
+    pltpu.make_async_copy(sent.at[sent_away], sent.at[sent_away], out_sem).wait()
+    pltpu.make_async_copy(answer.at[sent_away], answer.at[sent_away], ret_send).wait()
+    for c in range(chunks):
+        ring_copy(y, c, everything, right, 0).wait_send()
+        ring_copy(y, c, everything, left, 1).wait_send()
+        ring_copy(left, c, low, right, 2).wait_send()
+        ring_copy(right, c, high, left, 3).wait_send()
+        for step in range(1, ring):
+            hidden_copy(c, (y + step) % ring).wait_send()
+
+
+def expert_layer(moe_tiles, resid_tiles, token_of, slot_of, gates, w_gate, w_up, w_down, wd_all):
+    ring = lax.axis_size("exp")
+    planes, members = ctx_grid(lax.axis_size("ctx"))
+    slots = token_of.shape[0]
+    cell = slots // (planes * members)
+    groups, lanes = moe_tiles.shape[1:]
+    model_width = groups * lanes
+    hidden = w_gate.shape[1]
+    chunks, chunk_rows = planes // 2, 2 * members * cell
+    vmem, smem, anywhere = (
+        pl.BlockSpec(memory_space=pltpu.VMEM),
+        pl.BlockSpec(memory_space=pltpu.SMEM),
+        pl.BlockSpec(memory_space=pl.ANY),
+    )
+    tiles = pltpu.VMEM((slots, groups, lanes), jnp.bfloat16)
+    dma = pltpu.SemaphoreType.DMA
+    return pl.pallas_call(
+        functools.partial(expert_kernel, planes, members, ring, cell),
+        out_shape=jax.ShapeDtypeStruct(moe_tiles.shape, jnp.bfloat16),
+        in_specs=[vmem, vmem, smem, smem, smem, anywhere, anywhere, anywhere, anywhere],
+        out_specs=vmem,
+        scratch_shapes=[
+            tiles,
+            tiles,
+            pltpu.VMEM((ring, slots, model_width), jnp.bfloat16),
+            pltpu.VMEM((chunks, ring, chunk_rows, hidden), jnp.bfloat16),
+            pltpu.VMEM((chunks, ring, chunk_rows, hidden), jnp.bfloat16),
+            tiles,
+            tiles,
+            pltpu.VMEM((model_width, 2 * hidden), jnp.bfloat16),
+            pltpu.VMEM((ring, model_width, hidden), jnp.bfloat16),
+            dma((1,)),
+            dma((2 + ring,)),
+            dma,
+            dma((chunks,)),
+            dma((4, chunks)),
+            dma((4, chunks)),
+            dma((chunks, ring)),
+            dma((chunks, ring)),
+            dma,
+            dma,
+        ],
+        compiler_params=pltpu.CompilerParams(
+            collective_id=2, has_side_effects=True, vmem_limit_bytes=60 * 1024 * 1024
+        ),
+        name="experts",
+    )(moe_tiles, resid_tiles, token_of, slot_of, gates, w_gate, w_up, w_down, wd_all)
 
 
 def on_device(
@@ -127,40 +457,22 @@
     ).astype(jnp.float32)
     residual_rows = (tokens.astype(jnp.float32) + head_total).astype(jnp.bfloat16)
     moe_in = rms_rows(residual_rows, ffn_gain).astype(jnp.bfloat16)
-    slots = block_slots(indices, expert_count, capacity)
-    slot_ids = jnp.arange(expert_count * capacity, dtype=jnp.int32)
-    matched = slot_ids[:, None, None] == slots[None]
-    dispatch_table = jnp.any(matched, axis=2).astype(jnp.bfloat16)
-    combine_table = jnp.sum(
-        jnp.where(matched, gates[None].astype(jnp.float32), 0.0), axis=2
-    ).T.astype(jnp.bfloat16)
-    outgoing = jnp.dot(dispatch_table, moe_in, preferred_element_type=jnp.float32).astype(
-        jnp.bfloat16
-    )
-    outgoing = outgoing.reshape(ctx_count, local_experts, capacity, model_width)
-    piece = lax.all_gather(
-        lax.all_to_all(outgoing, "ctx", split_axis=0, concat_axis=0, tiled=True)[None],
-        "exp",
-        axis=0,
-        tiled=True,
-    )
-    gate_rows = jnp.einsum("xsepd,edf->xsepf", piece, w_gate, preferred_element_type=jnp.float32)
-    up_rows = jnp.einsum("xsepd,edf->xsepf", piece, w_up, preferred_element_type=jnp.float32)
-    hidden_rows = (jax.nn.silu(gate_rows) * up_rows).astype(jnp.bfloat16)
-    part = hidden_rows
-    summed = lax.psum_scatter(
-        rounded(
-            jnp.einsum("xsepf,edf->xsepd", part, w_down, preferred_element_type=jnp.float32)
-        ).astype(jnp.bfloat16),
-        "exp",
-        scatter_dimension=0,
-        tiled=True,
-    ).astype(jnp.float32)
-    expert_rows_out = summed[0].astype(jnp.bfloat16)
-    returned = lax.all_to_all(expert_rows_out, "ctx", split_axis=0, concat_axis=0, tiled=True)
-    returned = returned.reshape(expert_count * capacity, model_width)
-    moe_total = jnp.dot(combine_table, returned, preferred_element_type=jnp.float32)
-    return (residual_rows.astype(jnp.float32) + moe_total).astype(jnp.bfloat16)
+    planes, members = ctx_grid(ctx_count)
+    slot_of, token_of = routing(indices, expert_count, capacity, planes, members)
+    tile = (tok_rows, model_width // LANES, LANES)
+    wd_all = lax.all_gather(w_down[0], "exp", axis=0)
+    mixed = expert_layer(
+        moe_in.reshape(tile),
+        residual_rows.reshape(tile),
+        token_of,
+        slot_of,
+        gates.reshape(-1).astype(jnp.float32),
+        w_gate[0],
+        w_up[0],
+        w_down[0],
+        wd_all,
+    )
+    return mixed.reshape(tok_rows, model_width)
 
 
 def solution(mesh):

time: 516 us -> 396 us (0.77)
  waiting for transfers between devices: 348 us -> 233 us
  Pallas kernels: 0 us -> 97.4 us
  blocking collectives: 60.5 us -> 0 us
  matrix products: 39.7 us -> 17.8 us
  starting transfers between devices: 11.4 us -> 0.31 us
  local copies, waits for them, and re-layouts: 17.5 us -> 8.65 us
    pallas_call x0 -> x1, Pallas kernels: none -> 97.4 us  [expert_layer(): pl.pallas_call(functools.partial(expert_kernel, planes, members, ring, ce...]
    all_to_all x1 -> x0, blocking collectives: 60.5 us -> none  [on_device(): lax.all_to_all(outgoing, 'ctx', split_axis=0, concat_axis=0, tiled=True)]
    reduce_scatter x1 -> x0, waiting for transfers between devices: 58.7 us -> none  [on_device(): lax.psum_scatter(rounded(jnp.einsum('xsepf,edf->xsepd', part, w_down, pre...]
    all_to_all x1 -> x0, waiting for transfers between devices: 49.6 us -> none  [on_device(): lax.all_to_all(expert_rows_out, 'ctx', split_axis=0, concat_axis=0, tiled...]
    dot_general x4 -> x0, matrix products: 21.8 us -> none  [the longest x1 11.2 us: on_device(): jnp.einsum('xsepf,edf->xsepd', part, w_down, preferred_element_type=jnp.f...]
    all_to_all x1 -> x0, starting transfers between devices: 11.1 us -> none  [on_device(): lax.all_to_all(expert_rows_out, 'ctx', split_axis=0, concat_axis=0, tiled...]
    all_gather x1, waiting for transfers between devices: 55.2 us -> 47.6 us  [on_device(): wd_all = lax.all_gather(w_down[0], 'exp', axis=0)]
    reshape x2 -> x1, local copies, waits for them, and re-layouts: 7.06 us -> 0.14 us  [routing(): flat = indices.reshape(-1)]
  transfers between devices with their start and end apart: 6 -> 4, of which waited for: 6 -> 4; matrix products, arithmetic and copies ran while one was open for 2% -> 3% of each run, Pallas kernels for 0% -> 0%
where the time goes in v1:
time: 396 us; the launch traced here: 392 us
  waiting for transfers between devices  233 us (59%)
  Pallas kernels  97.4 us (25%)
  other arithmetic  21.7 us (5%)
  matrix products  17.8 us (4%)
  between operations  13.3 us (3%)
  local copies, waits for them, and re-layouts  8.65 us (2%)
    pallas_call x1, Pallas kernels, expert_layer(): pl.pallas_call(functools.partial(expert_kernel, planes, members, ring, ce...  97.4 us
    all_gather x1, waiting for transfers between devices, carried_in(): gathered = lax.all_gather(array.astype(jnp.bfloat16), axis)  74.8 us
    reduce_scatter x1, waiting for transfers between devices, on_device(): lax.psum_scatter(rounded(jnp.dot(part, w_out, preferred_element_type=jnp....  74.2 us
    all_gather x1, waiting for transfers between devices, on_device(): wd_all = lax.all_gather(w_down[0], 'exp', axis=0)  47.6 us
    all_gather x1, waiting for transfers between devices, on_device(): lax.all_gather(normed, 'exp', axis=0, tiled=True)  35.8 us
    add x15, other arithmetic, add_states(): return earlier + later  14.5 us
  transfers between devices with their start and end apart: 4, of which 4 were waited for; matrix products, arithmetic and copies ran while one was open for 3% of the time, Pallas kernels for 0%

profile of v1, /device:TPU:39, one launch (start us, length us, event | category | flops | bytes accessed | tf_op | source)
XLA Modules:
  0.0 392.4 jit_solution(16856025610389244062)
XLA Ops:
  6.5 1.4 fusion.16
  7.9 2.0 fusion.18
  10.0 35.8 %all-gather.5.cloned.1.call-done = bf16[512,2048]{1,0:T(8,128)(2,1)} async-done(((bf16[128,2048]{1,0:T(8,128)(2,1)}), bf16[512,2048]{1,0:T(8,128)(2,1)}) %all-gather.5.cloned.1.call-update) | async-done | bytes 2097168 | tf_op jit(solution)/shard_map/all_gather | solution.py:401
  45.9 6.9 %fusion.6 = bf16[512,1536]{1,0:T(8,128)(2,1)S(1)} fusion(bf16[512,2048]{1,0:T(8,128)(2,1)} %all-gather.5.cloned.1.call-done, bf16[2048,512]{1,0:T(8,128)(2,1)} %param.19, bf16[2048,512]{1,0:T(8,128)(2,1)} %param.18, bf16[2048,512]{1,0:T(8,128)(2,1)} %param.17), kind=kOutput, calls=%fused_computation.8 | convolution fusion | flops 3240886272 | bytes 9961472 | tf_op jit(solution)/shard_map/dot_general | solution.py:400
  52.7 1.1 fusion.47
  53.9 0.2 copy.50
  54.1 1.2 reshape.164
  55.3 1.0 convolution_convert_fusion.1
  56.3 0.1 iota_compare_fusion
  56.4 1.2 reshape.163
  57.6 1.6 fusion.25
  59.2 3.8 fusion.11
  63.0 74.8 %all-gather.9.cloned.1.call-done = bf16[256,128,128]{2,1,0:T(8,128)(2,1)} async-done(((bf16[4,128,128]{2,1,0:T(8,128)(2,1)}), bf16[256,128,128]{2,1,0:T(8,128)(2,1)}) %all-gather.9.cloned.1.call-update) | async-done | bytes 8388624 | tf_op jit(solution)/shard_map/all_gather | solution.py:21
  137.8 14.9 %while.2 = (s32[]{:T(128)}, f32[4,128,128]{2,1,0:T(8,128)S(1)}, s32[]{:T(128)}, bf16[64,4,128,128]{3,2,1,0:T(8,128)(2,1)}, s32[]{:T(128)}, /*index=5*/s32[]{:T(128)}, s32[]{:T(128)}) while((s32[]{:T(128)}, f32[4,128,128]{2,1,0:T(8,128)S(1)}, s32[]{:T(128)}, bf16[64,4,128,128]{3,2,1,0:T(8,128)(2,1)}, s32[]{:T(128)}, /*index=5*/s32[]{:T(128)}, ...), condition=%wide.region_2.3_spmd, body=%wide.region_1.2_spmd.sunk | while | flops 131077 | bytes 655475 | solution.py:27
  137.9 1.0 convert_add_fusion.3
  138.9 1.0 convert_add_fusion.3
  139.8 1.0 convert_add_fusion.3
  140.8 1.0 convert_add_fusion.3
  141.8 1.0 convert_add_fusion.3
  142.8 1.0 convert_add_fusion.3
  143.8 1.0 convert_add_fusion.3
  144.8 1.0 convert_add_fusion.3
  145.8 1.0 convert_add_fusion.3
  146.8 1.0 convert_add_fusion.3
  147.8 1.0 convert_add_fusion.3
  148.8 1.0 convert_add_fusion.3
  149.8 1.0 convert_add_fusion.3
  150.8 1.0 convert_add_fusion.3
  151.7 1.0 convert_add_fusion.3
  152.7 1.9 multiply_reduce_fusion
  154.7 0.2 multiply_convert_fusion
  154.9 2.6 convolution_convert_fusion
  157.5 0.2 all-gather.7.cloned.1.call-start
  157.7 0.3 all-gather.7.cloned.1.call-update
  158.1 0.1 copy.44
  158.2 0.1 reshape.169
  158.4 0.1 copy.45
  158.5 0.7 reshape.172.gate_ref
  159.2 0.2 convert_reduce_fusion
  159.5 0.7 select_reduce_fusion.token_ref
  160.2 74.2 %reduce-scatter.2.cloned.1.call-done = bf16[128,2048]{1,0:T(8,128)(2,1)} async-done(((bf16[512,2048]{1,0:T(8,128)(2,1)}), bf16[128,2048]{1,0:T(8,128)(2,1)}) %reduce-scatter.2.cloned.1.call-update) | async-done | bytes 524304 | tf_op jit(solution)/shard_map/reduce_scatter | solution.py:452
  234.4 1.3 fusion.13
  235.7 1.3 fusion.46
  237.0 0.9 copy.53
  237.9 0.9 copy.54
  238.8 47.6 %all-gather.7.cloned.1.call-done.wdall_hbm = bf16[4,2048,256]{2,1,0:T(8,128)(2,1)} async-done(((bf16[1,2048,256]{2,1,0:T(8,128)(2,1)}), bf16[4,2048,256]{2,1,0:T(8,128)(2,1)}) %all-gather.7.cloned.1.call-update) | async-done | bytes 4194320 | tf_op jit(solution)/shard_map/all_gather | solution.py:463
  286.5 97.4 %experts.1 = bf16[128,16,128]{2,1,0:T(8,128)(2,1)} custom-call(bf16[128,16,128]{2,1,0:T(8,128)(2,1)} %bitcast.65, bf16[128,16,128]{2,1,0:T(8,128)(2,1)} %bitcast.66, s32[320]{0:T(512)} %select_reduce_fusion.token_ref, s32[256]{0:T(256)} %copy-done.3, f32[256]{0:T(256)} %reshape.172.gate_ref, bf16[2048,256]{1,0:T(8,128)(2,1)} %bitcast.70, ...), custom_call_target="tpu_custom_call" | custom-call | tf_op jit(solution)/shard_map/experts/pallas_call | solution.py:345
  383.9 2.0 copy.81
  (27 shorter events, 0.3 us)
Async XLA Ops:
  6.5 148.3 %copy-start = (bf16[512,2048]{1,0:T(8,128)(2,1)S(1)}, bf16[512,2048]{1,0:T(8,128)(2,1)}, u32[]{:S(2)}) copy-start(bf16[512,2048]{1,0:T(8,128)(2,1)} %param.21) | copy-start | bytes 6291460
  6.5 39.3 %all-gather.5.cloned.1.call-start = ((), (), s32[]{:S(2)}) async-start(), calls=%async_computation.1 | async-start | bytes 2621440 | tf_op jit(solution)/shard_map/all_gather | solution.py:401
  10.0 127.8 %all-gather.9.cloned.1.call-start = ((), (), s32[]{:S(2)}) async-start(), calls=%async_computation.4 | async-start | bytes 8519680 | tf_op jit(solution)/shard_map/all_gather | solution.py:21
  55.3 1.2 copy-start.2
  56.3 178.1 %reduce-scatter.2.cloned.1.call-start = ((), (), s32[]{:S(2)}) async-start(), calls=%async_computation.2 | async-start | bytes 2621440 | tf_op jit(solution)/shard_map/reduce_scatter | solution.py:452
  152.7 1.9 copy-start.5
  157.5 0.7 copy-start.6
  157.5 0.9 copy-start.7
  157.5 76.9 %copy-start.1 = (bf16[128,2048]{1,0:T(8,128)(2,1)S(1)}, bf16[128,2048]{1,0:T(8,128)(2,1)}, u32[]{:S(2)}) copy-start(bf16[128,2048]{1,0:T(8,128)(2,1)} %param.15) | copy-start | bytes 1572868
  157.5 78.2 %copy-start.4 = (f32[2048]{0:T(1024)S(1)}, f32[2048]{0:T(1024)}, u32[]{:S(2)}) copy-start(f32[2048]{0:T(1024)} %param.22) | copy-start | bytes 24580
  157.5 129.0 %all-gather.7.cloned.1.call-start = ((), (), s32[]{:S(2)}) async-start(), calls=%async_computation.3 | async-start | bytes 5242880 | tf_op jit(solution)/shard_map/all_gather | solution.py:463
  159.4 78.5 %copy-start.3 = (s32[256]{0:T(256)}, s32[256]{0:T(256)S(1)}, u32[]{:S(2)}) copy-start(s32[256]{0:T(256)S(1)} %get-tuple-element.66.slot_ref) | copy-start | bytes 3076
Sparse Core Ops, SparseCore 0:
  10.1 35.7 all-gather.4
  56.4 81.3 all-gather.8
  157.6 76.7 reduce-scatter.1
  236.0 50.4 all-gather.6

commit v2 on v1

--- a/solution.py
+++ b/solution.py
@@ -8,47 +8,17 @@
 from jax.sharding import PartitionSpec as P
 
 HD = 128
-BLK = 512
 LANES = 128
 MESH = pl.DeviceIdType.MESH
 
 
 epsilon = 1e-06
-
-
-def carried_in(array, axis, join, neutral):
-    place = lax.axis_index(axis)
-    gathered = lax.all_gather(array.astype(jnp.bfloat16), axis)
-    state = jnp.zeros_like(array) + jnp.asarray(neutral, array.dtype)
-
-    def one(turn, state):
-        return join(state, lax.dynamic_index_in_dim(gathered, turn, 0, False).astype(array.dtype))
-
-    return lax.fori_loop(0, place, one, state)
 
 
 def rms_rows(values, gain):
     widened = values.astype(jnp.float32)
     mean_square = jnp.mean(widened * widened, axis=-1, keepdims=True)
     return widened * lax.rsqrt(mean_square + epsilon) * gain
-
-
-def rounded(values):
-    return lax.optimization_barrier(values.astype(jnp.bfloat16)).astype(jnp.float32)
-
-
-def block_slots(picked, expert_count, capacity):
-    flat_ids = picked.reshape(-1)
-    chosen = (flat_ids[:, None] == jnp.arange(expert_count, dtype=jnp.int32)[None, :]).astype(
-        jnp.int32
-    )
-    earlier = jnp.cumsum(chosen, axis=0) - chosen
-    position = jnp.sum(earlier * chosen, axis=1)
-    return (flat_ids * capacity + position).reshape(picked.shape)
-
-
-def add_states(earlier, later):
-    return earlier + later
 
 
 def ctx_grid(count):
@@ -97,7 +67,7 @@
     wg_hbm,
     wu_hbm,
     wd_hbm,
-    wdall_hbm,
+    near_hbm,
     out_ref,
     sent,
     got,
@@ -108,7 +78,6 @@
     back,
     wgu,
     wd,
-    local_sem,
     weight_sem,
     out_sem,
     in_sem,
@@ -118,6 +87,8 @@
     hid_recv,
     ret_send,
     ret_recv,
+    far_send,
+    far_recv,
 ):
     here = lax.axis_index("ctx")
     y = lax.axis_index("exp")
@@ -136,10 +107,9 @@
         pltpu.make_async_copy(wu_hbm, wgu.at[:, pl.ds(width, width)], weight_sem.at[1]),
         pltpu.make_async_copy(wd_hbm, wd.at[y], weight_sem.at[2]),
     ]
-    for step in range(1, ring):
-        other = (y + step) % ring
+    for side, other in enumerate((left, right)):
         loads.append(
-            pltpu.make_async_copy(wdall_hbm.at[other], wd.at[other], weight_sem.at[2 + step])
+            pltpu.make_async_copy(near_hbm.at[side], wd.at[other], weight_sem.at[3 + side])
         )
     for load in loads:
         load.start()
@@ -157,6 +127,18 @@
     for step in range(1, ring):
         pl.semaphore_signal(
             barrier, inc=1, device_id=(here, (y + step) % ring), device_id_type=MESH
+        )
+
+    def far_copy(side):
+        owner, target = ((left, right), (right, left))[side]
+        part = pl.ds(side * half, half)
+        return pltpu.make_async_remote_copy(
+            src_ref=near_hbm.at[side, part],
+            dst_ref=wd.at[owner, part],
+            send_sem=far_send.at[side],
+            recv_sem=far_recv.at[side],
+            device_id=(here, target),
+            device_id_type=MESH,
         )
 
     def pick(slot, carry):
@@ -182,6 +164,8 @@
         lax.fori_loop(k * plane_rows, (k + 1) * plane_rows, pick, 0, unroll=8)
         if k == 0:
             pl.semaphore_wait(barrier, everyone - 1 + ring - 1)
+            far_copy(0).start()
+            far_copy(1).start()
             own = pl.ds(m * cell, cell)
             pltpu.make_async_copy(sent.at[own], got.at[own], in_sem.at[0]).start()
             lax.fori_loop(1, members, to_plane(k), 0)
@@ -297,6 +281,8 @@
         if c - 3 == 0:
             for load in loads[2:]:
                 load.wait()
+            far_copy(0).wait_recv()
+            far_copy(1).wait_recv()
         if 0 <= c - 3 < chunks:
             contract(c - 3)
 
@@ -314,6 +300,8 @@
 
     lax.fori_loop(0, out_ref.shape[0], blend, 0, unroll=4)
 
+    far_copy(0).wait_send()
+    far_copy(1).wait_send()
     sent_away = pl.ds(0, total_rows - cell)
     pltpu.make_async_copy(sent.at[sent_away], sent.at[sent_away], out_sem).wait()
     pltpu.make_async_copy(answer.at[sent_away], answer.at[sent_away], ret_send).wait()
@@ -326,7 +314,7 @@
             hidden_copy(c, (y + step) % ring).wait_send()
 
 
-def expert_layer(moe_tiles, resid_tiles, token_of, slot_of, gates, w_gate, w_up, w_down, wd_all):
+def expert_layer(moe_tiles, resid_tiles, token_of, slot_of, gates, w_gate, w_up, w_down, near):
     ring = lax.axis_size("exp")
     planes, members = ctx_grid(lax.axis_size("ctx"))
     slots = token_of.shape[0]
@@ -357,8 +345,7 @@
             tiles,
             pltpu.VMEM((model_width, 2 * hidden), jnp.bfloat16),
             pltpu.VMEM((ring, model_width, hidden), jnp.bfloat16),
-            dma((1,)),
-            dma((2 + ring,)),
+            dma((5,)),
             dma,
             dma((chunks,)),
             dma((4, chunks)),
@@ -367,12 +354,388 @@
             dma((chunks, ring)),
             dma,
             dma,
+            dma((2,)),
+            dma((2,)),
         ],
         compiler_params=pltpu.CompilerParams(
             collective_id=2, has_side_effects=True, vmem_limit_bytes=60 * 1024 * 1024
         ),
         name="experts",
-    )(moe_tiles, resid_tiles, token_of, slot_of, gates, w_gate, w_up, w_down, wd_all)
+    )(moe_tiles, resid_tiles, token_of, slot_of, gates, w_gate, w_up, w_down, near)
+
+
+def attention_kernel(
+    planes,
+    members,
+    ring,
+    tokens_ref,
+    norm_gain_ref,
+    head_gain_ref,
+    ffn_gain_ref,
+    wq_hbm,
+    wk_hbm,
+    wv_hbm,
+    wo_hbm,
+    wd_hbm,
+    moe_ref,
+    resid_ref,
+    near_hbm,
+    wqkv,
+    wo,
+    normed,
+    qkv,
+    state,
+    plane_states,
+    plane_total,
+    totals,
+    earlier_out,
+    earlier,
+    inside,
+    heads,
+    parts,
+    via,
+    landed,
+    weight_sem,
+    ring_send,
+    ring_recv,
+    near_send,
+    near_recv,
+    scan_send,
+    scan_recv,
+    part_send,
+    part_recv,
+):
+    here = lax.axis_index("ctx")
+    y = lax.axis_index("exp")
+    z, m = here // members, here % members
+    right, left, across = (y + 1) % ring, (y + ring - 1) % ring, (y + 2) % ring
+    rows, model_width = tokens_ref.shape
+    width = wq_hbm.shape[1]
+    local_heads = width // HD
+    block = ring * rows
+    piece = state.shape[1]
+    per_head = HD // piece
+
+    loads = [
+        pltpu.make_async_copy(w, wqkv.at[:, pl.ds(i * width, width)], weight_sem.at[i])
+        for i, w in enumerate((wq_hbm, wk_hbm, wv_hbm))
+    ]
+    loads.append(pltpu.make_async_copy(wo_hbm, wo, weight_sem.at[3]))
+    for load in loads:
+        load.start()
+
+    barrier = pltpu.get_barrier_semaphore()
+    for step in range(1, ring):
+        pl.semaphore_signal(
+            barrier, inc=1, device_id=(here, (y + step) % ring), device_id_type=MESH
+        )
+
+    def plane_mate(step):
+        return (m + step) % members
+
+    def greet_mate(step, carry):
+        pl.semaphore_signal(
+            barrier, inc=1, device_id=(z * members + plane_mate(step), y), device_id_type=MESH
+        )
+        return carry
+
+    def greet_plane(step, carry):
+        pl.semaphore_signal(
+            barrier,
+            inc=1,
+            device_id=(((z + step) % planes) * members + m, y),
+            device_id_type=MESH,
+        )
+        return carry
+
+    lax.fori_loop(1, members, greet_mate, 0)
+    lax.fori_loop(1, planes, greet_plane, 0)
+
+    normed[y] = rms_rows(tokens_ref[...], norm_gain_ref[...]).astype(jnp.bfloat16)
+    pl.semaphore_wait(barrier, ring - 1 + members - 1 + planes - 1)
+
+    low, high = pl.ds(0, rows // 2), pl.ds(rows // 2, rows // 2)
+
+    def ring_copy(owner, part, target, kind):
+        return pltpu.make_async_remote_copy(
+            src_ref=normed.at[owner, part],
+            dst_ref=normed.at[owner, part],
+            send_sem=ring_send.at[kind],
+            recv_sem=ring_recv.at[kind],
+            device_id=(here, target),
+            device_id_type=MESH,
+        )
+
+    ring_copy(y, low, right, 0).start()
+    ring_copy(y, high, left, 1).start()
+    ring_copy(y, high, right, 2).start()
+    ring_copy(y, low, left, 3).start()
+
+    def near_copy(target, kind):
+        return pltpu.make_async_remote_copy(
+            src_ref=wd_hbm,
+            dst_ref=near_hbm.at[kind],
+            send_sem=near_send.at[kind],
+            recv_sem=near_recv.at[kind],
+            device_id=(here, target),
+            device_id_type=MESH,
+        )
+
+    def project(owner):
+        qkv[owner] = jnp.dot(
+            normed[owner], wqkv[...], preferred_element_type=jnp.float32
+        ).astype(jnp.bfloat16)
+
+    for load in loads[:3]:
+        load.wait()
+    project(y)
+    ring_copy(left, low, right, 0).wait_recv()
+    ring_copy(left, low, right, 4).start()
+    ring_copy(right, high, left, 1).wait_recv()
+    ring_copy(right, high, left, 5).start()
+    near_copy(right, 0).start()
+    near_copy(left, 1).start()
+    ring_copy(left, high, right, 2).wait_recv()
+    project(left)
+    ring_copy(right, low, left, 3).wait_recv()
+    project(right)
+    ring_copy(across, low, right, 4).wait_recv()
+    ring_copy(across, high, left, 5).wait_recv()
+    project(across)
+
+    def columns(kind, head):
+        return pl.ds(kind * width + head * HD, HD)
+
+    for head in range(local_heads):
+        head_state = lax.dot_general(
+            qkv[:, :, columns(1, head)].reshape(block, HD),
+            qkv[:, :, columns(2, head)].reshape(block, HD),
+            (((0,), (0,)), ((), ())),
+            preferred_element_type=jnp.float32,
+        )
+        state[head * per_head : (head + 1) * per_head] = head_state.astype(jnp.bfloat16).reshape(
+            per_head, piece, HD
+        )
+
+    def to_mates(source, landing, kind):
+        def one(step, carry):
+            t = plane_mate(step)
+            pltpu.make_async_remote_copy(
+                src_ref=source.at[t],
+                dst_ref=landing.at[m],
+                send_sem=scan_send.at[kind],
+                recv_sem=scan_recv.at[kind],
+                device_id=(z * members + t, y),
+                device_id_type=MESH,
+            ).start()
+            return carry
+
+        lax.fori_loop(1, members, one, 0)
+
+    def all_of(buffer, count, semaphore):
+        part = buffer.at[pl.ds(0, count)]
+        pltpu.make_async_copy(part, part, semaphore).wait()
+
+    def within(head):
+        tall = block // 2
+        keys = qkv[:, :, columns(1, head)].reshape(block, HD)
+        values = qkv[:, :, columns(2, head)].reshape(block, HD)
+        queries = qkv[:, :, columns(0, head)].reshape(block, HD)
+        for i in range(2):
+            reach = (i + 1) * tall
+            scores = lax.dot_general(
+                queries[i * tall : reach],
+                keys[:reach],
+                (((1,), (1,)), ((), ())),
+                preferred_element_type=jnp.float32,
+            )
+            at = lax.broadcasted_iota(jnp.int32, (tall, reach), 0) + i * tall
+            of = lax.broadcasted_iota(jnp.int32, (tall, reach), 1)
+            masked = jnp.where(of <= at, scores, 0.0).astype(jnp.bfloat16)
+            inside[head, i * tall : reach] = jnp.dot(
+                masked, values[:reach], preferred_element_type=jnp.float32
+            )
+
+    to_mates(state, plane_states, 0)
+    plane_states[m] = state[m]
+    within(0)
+    all_of(plane_states, members - 1, scan_recv.at[0])
+    running = jnp.zeros((piece, HD), jnp.float32)
+    before = []
+    for t in range(members):
+        before.append(running)
+        running = running + plane_states[t].astype(jnp.float32)
+    plane_total[...] = running.astype(jnp.bfloat16)
+
+    def to_planes(step, carry):
+        pltpu.make_async_remote_copy(
+            src_ref=plane_total,
+            dst_ref=totals.at[z],
+            send_sem=scan_send.at[1],
+            recv_sem=scan_recv.at[1],
+            device_id=(((z + step) % planes) * members + m, y),
+            device_id_type=MESH,
+        ).start()
+        return carry
+
+    lax.fori_loop(1, planes, to_planes, 0)
+    totals[z] = plane_total[...]
+    within(1)
+    within(2)
+    all_of(totals, planes - 1, scan_recv.at[1])
+    base = jnp.zeros((piece, HD), jnp.float32)
+    for other in range(planes):
+        base = base + jnp.where(other < z, totals[other].astype(jnp.float32), 0.0)
+    for t in range(members):
+        earlier_out[t] = (base + before[t]).astype(jnp.bfloat16)
+    to_mates(earlier_out, earlier, 2)
+    earlier[m] = earlier_out[m]
+    within(3)
+    all_of(earlier, members - 1, scan_recv.at[2])
+
+    for head in range(local_heads):
+        carried = jnp.dot(
+            qkv[:, :, columns(0, head)].reshape(block, HD),
+            earlier[head * per_head : (head + 1) * per_head].reshape(HD, HD),
+            preferred_element_type=jnp.float32,
+        )
+        gain = head_gain_ref[:, head * HD : (head + 1) * HD]
+        heads[:, :, head * HD : (head + 1) * HD] = (
+            rms_rows(inside[head] + carried, gain).astype(jnp.bfloat16).reshape(ring, rows, HD)
+        )
+
+    def share(target):
+        return jnp.dot(heads[target], wo[...], preferred_element_type=jnp.float32).astype(
+            jnp.bfloat16
+        )
+
+    def part_copy(source, landing, target, kind):
+        return pltpu.make_async_remote_copy(
+            src_ref=source,
+            dst_ref=landing,
+            send_sem=part_send.at[kind],
+            recv_sem=part_recv.at[kind],
+            device_id=(here, target),
+            device_id_type=MESH,
+        )
+
+    def part_send_of(kind):
+        source, landing, target = (
+            (parts.at[0, low], via.at[0], right),
+            (parts.at[0, high], via.at[1], left),
+            (parts.at[1, high], landed.at[0, high], right),
+            (parts.at[2, low], landed.at[1, low], left),
+            (parts.at[1, low], landed.at[0, low], right),
+            (parts.at[2, high], landed.at[1, high], left),
+        )[kind]
+        return part_copy(source, landing, target, kind)
+
+    loads[3].wait()
+    parts[0] = share(across)
+    part_send_of(0).start()
+    part_send_of(1).start()
+    parts[1] = share(right)
+    part_send_of(2).start()
+    parts[2] = share(left)
+    part_send_of(3).start()
+    part_send_of(0).wait_recv()
+    parts[1, low] = (
+        parts[1, low].astype(jnp.float32) + via[0].astype(jnp.float32)
+    ).astype(jnp.bfloat16)
+    part_send_of(4).start()
+    part_send_of(1).wait_recv()
+    parts[2, high] = (
+        parts[2, high].astype(jnp.float32) + via[1].astype(jnp.float32)
+    ).astype(jnp.bfloat16)
+    part_send_of(5).start()
+    total = tokens_ref[...].astype(jnp.float32) + share(y).astype(jnp.float32)
+    for kind in range(2, 6):
+        part_send_of(kind).wait_recv()
+    residual = (
+        total + landed[0].astype(jnp.float32) + landed[1].astype(jnp.float32)
+    ).astype(jnp.bfloat16)
+    resid_ref[...] = residual.reshape(resid_ref.shape)
+    moe_ref[...] = (
+        rms_rows(residual, ffn_gain_ref[...]).astype(jnp.bfloat16).reshape(moe_ref.shape)
+    )
+
+    near_copy(right, 0).wait()
+    near_copy(left, 1).wait()
+    ring_copy(y, low, right, 0).wait_send()
+    ring_copy(y, high, left, 1).wait_send()
+    ring_copy(y, high, right, 2).wait_send()
+    ring_copy(y, low, left, 3).wait_send()
+    ring_copy(left, low, right, 4).wait_send()
+    ring_copy(right, high, left, 5).wait_send()
+    all_of(state, members - 1, scan_send.at[0])
+    all_of(totals, planes - 1, scan_send.at[1])
+    all_of(earlier_out, members - 1, scan_send.at[2])
+    for kind in range(6):
+        part_send_of(kind).wait_send()
+
+
+def attention_layer(
+    tokens, norm_gain, w_query, w_key, w_value, head_gain, w_out, ffn_gain, w_down
+):
+    ring = lax.axis_size("exp")
+    planes, members = ctx_grid(lax.axis_size("ctx"))
+    rows, model_width = tokens.shape
+    width = w_query.shape[1]
+    block = ring * rows
+    piece = width // members
+    vmem, anywhere = pl.BlockSpec(memory_space=pltpu.VMEM), pl.BlockSpec(memory_space=pl.ANY)
+    tile = jax.ShapeDtypeStruct((rows, model_width // LANES, LANES), jnp.bfloat16)
+    dma = pltpu.SemaphoreType.DMA
+
+    def half(*shape):
+        return pltpu.VMEM(shape, jnp.bfloat16)
+
+    return pl.pallas_call(
+        functools.partial(attention_kernel, planes, members, ring),
+        out_shape=(tile, tile, jax.ShapeDtypeStruct((2, *w_down.shape), jnp.bfloat16)),
+        in_specs=[vmem] * 4 + [anywhere] * 5,
+        out_specs=(vmem, vmem, anywhere),
+        scratch_shapes=[
+            half(model_width, 3 * width),
+            half(width, model_width),
+            half(ring, rows, model_width),
+            half(ring, rows, 3 * width),
+            half(members, piece, HD),
+            half(members, piece, HD),
+            half(piece, HD),
+            half(planes, piece, HD),
+            half(members, piece, HD),
+            half(members, piece, HD),
+            pltpu.VMEM((width // HD, block, HD), jnp.float32),
+            half(ring, rows, width),
+            half(3, rows, model_width),
+            half(2, rows // 2, model_width),
+            half(2, rows, model_width),
+            dma((4,)),
+            dma((6,)),
+            dma((6,)),
+            dma((2,)),
+            dma((2,)),
+            dma((3,)),
+            dma((3,)),
+            dma((6,)),
+            dma((6,)),
+        ],
+        compiler_params=pltpu.CompilerParams(
+            collective_id=1, has_side_effects=True, vmem_limit_bytes=60 * 1024 * 1024
+        ),
+        name="attention",
+    )(
+        tokens,
+        norm_gain.reshape(1, -1),
+        head_gain.reshape(1, -1),
+        ffn_gain.reshape(1, -1),
+        w_query,
+        w_key,
+        w_value,
+        w_out,
+        w_down,
+    )
 
 
 def on_device(
@@ -392,85 +755,23 @@
 ):
     tok_rows, model_width = tokens.shape
     ctx_count = lax.axis_size("ctx")
-    local_experts = w_gate.shape[0]
-    expert_count = local_experts * ctx_count
+    expert_count = w_gate.shape[0] * ctx_count
     capacity = max(2, (5 * tok_rows + 2 * expert_count - 1) // (2 * expert_count))
-    normed = rms_rows(tokens, norm_gain).astype(jnp.bfloat16)
-    joined_weights = jnp.concatenate([w_query, w_key, w_value], axis=1)
-    projected = jnp.dot(
-        lax.all_gather(normed, "exp", axis=0, tiled=True),
-        joined_weights,
-        preferred_element_type=jnp.float32,
-    ).astype(jnp.bfloat16)
-    shard_rows = projected.shape[0]
-    local_width = w_query.shape[1]
-    local_heads = local_width // HD
-    block_count = shard_rows // BLK
-
-    def split_heads(columns):
-        return columns.reshape(block_count, BLK, local_heads, HD).transpose(0, 2, 1, 3)
-
-    query_blocks = split_heads(projected[:, :local_width])
-    key_blocks = split_heads(projected[:, local_width : 2 * local_width])
-    value_blocks = split_heads(projected[:, 2 * local_width :])
-    causal = jnp.tril(jnp.ones((BLK, BLK), dtype=bool))
-
-    def block_step(kv_state, block):
-        query_block, key_block, value_block = block
-        score_block = jnp.einsum(
-            "hqd,hkd->hqk", query_block, key_block, preferred_element_type=jnp.float32
-        )
-        masked = jnp.where(causal[None], score_block, 0.0).astype(jnp.bfloat16)
-        inside = jnp.einsum("hqk,hkd->hqd", masked, value_block, preferred_element_type=jnp.float32)
-        carried = jnp.einsum(
-            "hqd,hde->hqe",
-            query_block.astype(jnp.float32),
-            kv_state,
-            precision=lax.Precision.HIGHEST,
-        )
-        kv_state = kv_state + jnp.einsum(
-            "hkd,hke->hde", key_block, value_block, preferred_element_type=jnp.float32
-        )
-        return (kv_state, inside + carried)
-
-    local_state, inside_rows = lax.scan(
-        block_step,
-        jnp.zeros((local_heads, HD, HD), jnp.float32),
-        (query_blocks, key_blocks, value_blocks),
-    )
-    before = carried_in(local_state, "ctx", add_states, jnp.zeros_like(local_state))
-    carried_rows = jnp.einsum(
-        "bhqd,hde->bhqe", query_blocks.astype(jnp.float32), before, precision=lax.Precision.HIGHEST
-    )
-    attended = inside_rows + carried_rows
-    mean_square = jnp.mean(attended * attended, axis=-1, keepdims=True)
-    head_out = (
-        attended * lax.rsqrt(mean_square + epsilon) * head_gain.reshape(1, local_heads, 1, HD)
-    ).astype(jnp.bfloat16)
-    head_rows = head_out.transpose(0, 2, 1, 3).reshape(shard_rows, local_width)
-    part = head_rows
-    head_total = lax.psum_scatter(
-        rounded(jnp.dot(part, w_out, preferred_element_type=jnp.float32)).astype(jnp.bfloat16),
-        "exp",
-        scatter_dimension=0,
-        tiled=True,
-    ).astype(jnp.float32)
-    residual_rows = (tokens.astype(jnp.float32) + head_total).astype(jnp.bfloat16)
-    moe_in = rms_rows(residual_rows, ffn_gain).astype(jnp.bfloat16)
     planes, members = ctx_grid(ctx_count)
     slot_of, token_of = routing(indices, expert_count, capacity, planes, members)
-    tile = (tok_rows, model_width // LANES, LANES)
-    wd_all = lax.all_gather(w_down[0], "exp", axis=0)
+    moe_tiles, resid_tiles, near = attention_layer(
+        tokens, norm_gain, w_query, w_key, w_value, head_gain, w_out, ffn_gain, w_down[0]
+    )
     mixed = expert_layer(
-        moe_in.reshape(tile),
-        residual_rows.reshape(tile),
+        moe_tiles,
+        resid_tiles,
         token_of,
         slot_of,
         gates.reshape(-1).astype(jnp.float32),
         w_gate[0],
         w_up[0],
         w_down[0],
-        wd_all,
+        near,
     )
     return mixed.reshape(tok_rows, model_width)
 

time: 396 us -> 174 us (0.44)
  waiting for transfers between devices: 233 us -> 0 us
  Pallas kernels: 97.4 us -> 169 us
  other arithmetic: 21.7 us -> 0.94 us
  matrix products: 17.8 us -> 0 us
  between operations: 13.3 us -> 0.04 us
  local copies, waits for them, and re-layouts: 8.65 us -> 4.4 us
    all_gather x3 -> x0, waiting for transfers between devices: 158 us -> none  [the longest x1 74.8 us: carried_in(): gathered = lax.all_gather(array.astype(jnp.bfloat16), axis)]
    reduce_scatter x1 -> x0, waiting for transfers between devices: 74.2 us -> none  [on_device(): lax.psum_scatter(rounded(jnp.dot(part, w_out, preferred_element_type=jnp....]
    pallas_call x0 -> x1, Pallas kernels: none -> 67.9 us  [attention_layer(): pl.pallas_call(functools.partial(attention_kernel, planes, members, ring)...]
    dot_general x6 -> x0, matrix products: 17.8 us -> none  [the longest x1 6.87 us: on_device(): jnp.dot(lax.all_gather(normed, 'exp', axis=0, tiled=True), joined_weights...]
    add x15 -> x0, other arithmetic: 14.5 us -> none  [add_states(): return earlier + later]
  transfers between devices with their start and end apart: 4 -> 0, of which waited for: 4 -> 0; matrix products, arithmetic and copies ran while one was open for 3% -> 0% of each run, Pallas kernels for 0% -> 0%
where the time goes in v2:
time: 174 us
  Pallas kernels  169 us (97%)
  local copies, waits for them, and re-layouts  4.4 us (3%)
    pallas_call x1, Pallas kernels, expert_layer(): pl.pallas_call(functools.partial(expert_kernel, planes, members, ring, ce...  101 us
    pallas_call x1, Pallas kernels, attention_layer(): pl.pallas_call(functools.partial(attention_kernel, planes, members, ring)...  67.9 us

profile of v2, /device:TPU:39, one launch (start us, length us, event | category | flops | bytes accessed | tf_op | source)
XLA Modules:
  0.0 174.2 jit_solution(13820902225577574063)
XLA Ops:
  0.0 0.8 copy.16
  0.8 0.1 reshape.111
  0.9 0.2 convert_reduce_fusion
  1.1 0.0 copy-start
  1.2 0.7 select_reduce_fusion.token_ref
  1.9 0.8 copy.17
  2.6 0.7 reshape.113.gate_ref
  3.4 67.9 %attention.1 = (bf16[128,16,128]{2,1,0:T(8,128)(2,1)}, bf16[128,16,128]{2,1,0:T(8,128)(2,1)}, bf16[2,2048,256]{2,1,0:T(8,128)(2,1)}) custom-call(bf16[128,2048]{1,0:T(8,128)(2,1)} %tokens_ref.1, f32[1,2048]{1,0:T(1,128)} %bitcast.15, f32[1,512]{1,0:T(1,128)} %bitcast.17, f32[1,2048]{1,0:T(1,128)} %bitcast.16, bf16[2048,512]{1,0:T(8,128)(2,1)} %wq_hbm.1, ...), custom_call_target="tpu_custom_call" | custom-call | tf_op jit(solution)/shard_map/attention/pallas_call | solution.py:693
  71.3 0.0 copy-done
  71.3 100.9 %experts.1 = bf16[128,16,128]{2,1,0:T(8,128)(2,1)} custom-call(bf16[128,16,128]{2,1,0:T(8,128)(2,1)} %get-tuple-element.8.moe_ref, bf16[128,16,128]{2,1,0:T(8,128)(2,1)} %get-tuple-element.9.resid_ref, s32[320]{0:T(512)} %select_reduce_fusion.token_ref, s32[256]{0:T(256)} %copy-done, f32[256]{0:T(256)} %reshape.113.gate_ref, bf16[2048,256]{1,0:T(8,128)(2,1)} %bitcast.13, ...), custom_call_target="tpu_custom_call" | custom-call | tf_op jit(solution)/shard_map/experts/pallas_call | solution.py:333
  172.2 2.0 %copy.20 = bf16[16,8,16,128]{3,1,2,0:T(8,128)(2,1)} copy(bf16[16,8,16,128]{3,2,1,0:T(8,128)(2,1)} %bitcast.12) | data formatting | bytes 1048576
  (1 shorter events, 0.0 us)
Async XLA Ops:
  1.1 70.2 %copy-start = (s32[256]{0:T(256)}, s32[256]{0:T(256)S(1)}, u32[]{:S(2)}) copy-start(s32[256]{0:T(256)S(1)} %get-tuple-element.12.slot_ref) | copy-start | bytes 3076

commit v3 on v2

--- a/solution.py
+++ b/solution.py
@@ -37,6 +37,7 @@
     turn = jnp.where(
         away == 0, 0, jnp.where(away <= planes // 2, 2 * away - 1, 2 * (planes - away))
     )
+    turn = planes - 1 - turn
     slot_of = (turn * members + flat % members) * capacity + position
     slot_ids = jnp.arange(expert_count * capacity, dtype=jnp.int32)
     token_of = jnp.sum(
@@ -51,7 +52,7 @@
         order.append(far)
         if len(order) < planes:
             order.append(planes - far)
-    return order
+    return order[::-1]
 
 
 def expert_kernel(
@@ -166,8 +167,9 @@
             pl.semaphore_wait(barrier, everyone - 1 + ring - 1)
             far_copy(0).start()
             far_copy(1).start()
-            own = pl.ds(m * cell, cell)
-            pltpu.make_async_copy(sent.at[own], got.at[own], in_sem.at[0]).start()
+        if order[k] == 0:
+            own = pl.ds(k * plane_rows + m * cell, cell)
+            pltpu.make_async_copy(sent.at[own], got.at[own], in_sem.at[k // 2]).start()
             lax.fori_loop(1, members, to_plane(k), 0)
         else:
             lax.fori_loop(0, members, to_plane(k), 0)
@@ -261,8 +263,8 @@
                 ).start()
                 return carry
 
-            if k == 0:
-                own = pl.ds(m * cell, cell)
+            if order[k] == 0:
+                own = pl.ds(k * plane_rows + m * cell, cell)
                 pltpu.make_async_copy(answer.at[own], back.at[own], ret_recv).start()
                 lax.fori_loop(1, members, one, 0)
             else:

time: 174 us -> 177 us (1.017); the launches traced: 174 us -> 174 us
  no operation moved by 1% of the time
where the time goes in v3:
time: 177 us; the launch traced here: 174 us
  Pallas kernels  169 us (95%)
  local copies, waits for them, and re-layouts  4.4 us (2%)
    pallas_call x1, Pallas kernels, expert_layer(): pl.pallas_call(functools.partial(expert_kernel, planes, members, ring, ce...  101 us
    pallas_call x1, Pallas kernels, attention_layer(): pl.pallas_call(functools.partial(attention_kernel, planes, members, ring)...  67.9 us

profile of v3, /device:TPU:39, one launch (start us, length us, event | category | flops | bytes accessed | tf_op | source)
XLA Modules:
  0.0 174.0 jit_solution(7787885104489524480)
XLA Ops:
  0.0 0.8 copy.16
  0.8 0.1 reshape.112
  0.9 0.2 convert_reduce_fusion
  1.1 0.0 copy-start
  1.2 0.7 select_reduce_fusion.token_ref
  1.9 0.8 copy.17
  2.7 0.7 reshape.114.gate_ref
  3.4 67.9 %attention.1 = (bf16[128,16,128]{2,1,0:T(8,128)(2,1)}, bf16[128,16,128]{2,1,0:T(8,128)(2,1)}, bf16[2,2048,256]{2,1,0:T(8,128)(2,1)}) custom-call(bf16[128,2048]{1,0:T(8,128)(2,1)} %tokens_ref.1, f32[1,2048]{1,0:T(1,128)} %bitcast.15, f32[1,512]{1,0:T(1,128)} %bitcast.17, f32[1,2048]{1,0:T(1,128)} %bitcast.16, bf16[2048,512]{1,0:T(8,128)(2,1)} %wq_hbm.1, ...), custom_call_target="tpu_custom_call" | custom-call | tf_op jit(solution)/shard_map/attention/pallas_call | solution.py:695
  71.3 0.0 copy-done
  71.3 100.7 %experts.1 = bf16[128,16,128]{2,1,0:T(8,128)(2,1)} custom-call(bf16[128,16,128]{2,1,0:T(8,128)(2,1)} %get-tuple-element.8.moe_ref, bf16[128,16,128]{2,1,0:T(8,128)(2,1)} %get-tuple-element.9.resid_ref, s32[320]{0:T(512)} %select_reduce_fusion.token_ref, s32[256]{0:T(256)} %copy-done, f32[256]{0:T(256)} %reshape.114.gate_ref, bf16[2048,256]{1,0:T(8,128)(2,1)} %bitcast.13, ...), custom_call_target="tpu_custom_call" | custom-call | tf_op jit(solution)/shard_map/experts/pallas_call | solution.py:335
  172.0 2.0 %copy.20 = bf16[16,8,16,128]{3,1,2,0:T(8,128)(2,1)} copy(bf16[16,8,16,128]{3,2,1,0:T(8,128)(2,1)} %bitcast.12) | data formatting | bytes 1048576
  (1 shorter events, 0.0 us)
Async XLA Ops:
  1.1 70.2 %copy-start = (s32[256]{0:T(256)}, s32[256]{0:T(256)S(1)}, u32[]{:S(2)}) copy-start(s32[256]{0:T(256)S(1)} %get-tuple-element.12.slot_ref) | copy-start | bytes 3076
